TPU v7x, 256 devices: a whole 4x4x8 slice. The times are simulated.
256 devices in a mesh: grp: 8 (over y, core), row: 32 (over z, x).
Axes of the slice: x: 4, y: 4, z: 8, core: 2. Of those that a mesh axis runs over, the one named last changes fastest.
Arguments:
- features: bfloat16 [524288, 256], P(('grp', 'row')), may hold values from -6 to 6
- cotangent: bfloat16 [524288, 256], P(('grp', 'row')), may hold values from -6 to 6
- self_weight: bfloat16 [256, 256], replicated, may hold values from -0.375 to 0.375
- neighbor_weight: bfloat16 [256, 256], replicated, may hold values from -0.375 to 0.375
- tile_values: bfloat16 [256, 64, 128, 128], P(('grp', 'row')), may hold values from 0 to 1
- tile_index: int32 [256, 64, 2], P(('grp', 'row')), may hold values from 0 to 15
- hub_adjacency: bfloat16 [524288, 1024], P(('grp', 'row')), may hold values from 0 to 1
- hub_owner: int32 [8, 8], P('grp'), may hold values from 0 to 31
- send_rows: int32 [256, 8, 64], P(('grp', 'row')), may hold values from 0 to 2047
- cut_adjacency: bfloat16 [524288, 512], P(('grp', 'row')), may hold values from 0 to 1
- degrees: int32 [524288], P(('grp', 'row')), may hold values from 1024 to 2047
Outputs:
- hidden: bfloat16 [524288, 256], P(('grp', 'row'))
- grad_features: bfloat16 [524288, 256], P(('grp', 'row'))
- grad_self: float32 [256, 256], replicated
- grad_neighbor: float32 [256, 256], replicated
Inputs may be any that keep to these rules, and one draw needn't show every extreme that they name: `send_rows`: rows may repeat.
All inputs are finite; a program needn't handle non-finite values.
Results may differ from a plain program's by a relative error of at most 0.014.
Values may be sent and summed in bfloat16 or wider, within the bound.
A program may use at most 128 MiB of HBM per device.

v0:
```python
import jax
import jax.numpy as jnp
from jax import lax
from jax.sharding import PartitionSpec as P

TILE = 128
HUB = 128


def spread(value, axis, root):
    mine = lax.axis_index(axis) == root
    return lax.psum(jnp.where(mine, value, jnp.zeros_like(value)), axis)


def on_device(
    features,
    cotangent,
    self_weight,
    neighbor_weight,
    tile_values,
    tile_index,
    hub_adjacency,
    hub_owner,
    send_rows,
    cut_adjacency,
    degrees,
):
    node_count, width = features.shape
    tile_total = node_count // TILE
    group_count = lax.axis_size("grp")
    section_count = hub_owner.shape[1]
    values = tile_values[0]
    index = tile_index[0]
    owners = hub_owner[0]
    blocks = features.reshape(tile_total, TILE, width)
    row_select = (index[:, 0][None, :] == jnp.arange(tile_total)[:, None]).astype(jnp.float32)
    col_select = (index[:, 1][None, :] == jnp.arange(tile_total)[:, None]).astype(jnp.float32)
    picked = blocks[index[:, 1]]
    product = jnp.einsum("lab,lbf->laf", values, picked, preferred_element_type=jnp.float32)
    local_sum = jnp.einsum(
        "nl,laf->naf", row_select, product, precision=lax.Precision.HIGHEST
    ).reshape(node_count, width)
    heads = features[:HUB]
    hub_sum = jnp.zeros((node_count, width), jnp.float32)
    for section in range(section_count):
        panel = spread(heads, "row", owners[section])
        hub_sum = hub_sum + jnp.dot(
            hub_adjacency[:, section * HUB : (section + 1) * HUB],
            panel,
            preferred_element_type=jnp.float32,
        )
    outgoing = features[send_rows[0]]
    arrived = lax.all_to_all(outgoing, "grp", split_axis=0, concat_axis=0, tiled=True)
    cut_sum = jnp.dot(
        cut_adjacency,
        arrived.reshape(group_count * outgoing.shape[1], width),
        preferred_element_type=jnp.float32,
    )
    scaling = lax.rsqrt(degrees.astype(jnp.float32))[:, None]
    aggregated = ((local_sum + hub_sum + cut_sum) * scaling).astype(jnp.bfloat16)
    before = jnp.dot(features, self_weight, preferred_element_type=jnp.float32) + jnp.dot(
        aggregated, neighbor_weight, preferred_element_type=jnp.float32
    )
    activated, pullback = jax.vjp(jax.nn.gelu, before)
    hidden = activated.astype(jnp.bfloat16)
    grad_before = pullback(cotangent.astype(jnp.float32))[0].astype(jnp.bfloat16)
    rows_dims = (((0,), (0,)), ((), ()))
    cols_dims = (((1,), (1,)), ((), ()))
    self_part = lax.dot_general(
        features, grad_before, rows_dims, preferred_element_type=jnp.float32
    )
    neighbor_part = lax.dot_general(
        aggregated, grad_before, rows_dims, preferred_element_type=jnp.float32
    )
    grad_self, grad_neighbor = lax.psum((self_part, neighbor_part), ("grp", "row"))
    grad_aggregate = (
        lax.dot_general(grad_before, neighbor_weight, cols_dims, preferred_element_type=jnp.float32)
        * scaling
    ).astype(jnp.bfloat16)
    grad_total = lax.dot_general(
        grad_before, self_weight, cols_dims, preferred_element_type=jnp.float32
    )
    agg_blocks = grad_aggregate.reshape(tile_total, TILE, width)[index[:, 0]]
    returned = jnp.einsum("lab,laf->lbf", values, agg_blocks, preferred_element_type=jnp.float32)
    grad_total = grad_total + jnp.einsum(
        "nl,lbf->nbf", col_select, returned, precision=lax.Precision.HIGHEST
    ).reshape(node_count, width)
    hub_terms = lax.dot_general(
        hub_adjacency, grad_aggregate, rows_dims, preferred_element_type=jnp.float32
    ).reshape(section_count, HUB, width)
    totals = lax.psum(hub_terms.astype(jnp.bfloat16), "row").astype(jnp.float32)
    owned = (owners == lax.axis_index("row")).astype(jnp.float32)
    hub_grad = jnp.einsum("s,shf->hf", owned, totals, precision=lax.Precision.HIGHEST)
    grad_total = grad_total.at[:HUB].add(hub_grad)
    back_rows = lax.dot_general(
        cut_adjacency, grad_aggregate, rows_dims, preferred_element_type=jnp.float32
    ).astype(jnp.bfloat16)
    back_rows = back_rows.reshape(group_count, -1, width)
    returned_rows = lax.all_to_all(back_rows, "grp", split_axis=0, concat_axis=0, tiled=True)
    scatter_table = (send_rows[0].reshape(-1)[None, :] == jnp.arange(node_count)[:, None]).astype(
        jnp.bfloat16
    )
    grad_total = grad_total + jnp.dot(
        scatter_table, returned_rows.reshape(-1, width), preferred_element_type=jnp.float32
    )
    return (hidden, grad_total.astype(jnp.bfloat16), grad_self, grad_neighbor)


def solution(mesh):
    in_specs = (
        P(("grp", "row"), None),
        P(("grp", "row"), None),
        P(),
        P(),
        P(("grp", "row"), None, None, None),
        P(("grp", "row"), None, None),
        P(("grp", "row"), None),
        P("grp", None),
        P(("grp", "row"), None, None),
        P(("grp", "row"), None),
        P(("grp", "row")),
    )
    out_specs = (P(("grp", "row"), None), P(("grp", "row"), None), P(), P())
    return jax.shard_map(
        on_device, mesh=mesh, in_specs=in_specs, out_specs=out_specs, check_vma=False
    )
```

profile of v0, /device:TPU:8, one launch (start us, length us, event | category | flops | bytes accessed | tf_op | source)
XLA Modules:
  0.0 638.3 jit_solution(11707294678581093016)
XLA Ops:
  7.2 0.0 copy-start
  7.2 0.0 copy-start.1
  7.2 0.8 compare_select_fusion
  8.1 0.1 reshape.124
  8.2 3.6 gather_fusion.1
  11.7 5.5 all-to-all-start
  17.3 0.6 fusion.52
  22.9 0.8 broadcast_select_fusion
  23.7 0.0 all-reduce.10.cloned.1.call-update
  23.7 0.0 all-reduce.8.cloned.1.call-start
  23.8 0.6 eq.97
  24.4 0.6 slice_bitcast_fusion
  25.0 2.8 gather_fusion
  27.8 6.8 %fusion.25 = f32[64,256,128]{2,1,0:T(8,128)} fusion(bf16[64,128,256]{2,1,0:T(8,128)(2,1)} %gather_fusion, bf16[1,64,128,128]{3,2,1,0:T(8,128)(2,1)S(1)} %copy-done), kind=kOutput, calls=%fused_computation.44 | convolution fusion | flops 536870912 | bytes 14680064 | tf_op jit(solution)/shard_map/lab,lbf->laf/dot_general | solution.py:39
  34.6 9.2 %copy.25 = f32[64,256,128]{1,0,2:T(8,128)} copy(f32[64,256,128]{2,1,0:T(8,128)} %fusion.25) | data formatting | bytes 16777216 | tf_op jit(solution)/shard_map/lab,lbf->laf/dot_general | solution.py:39
  43.8 5.2 fusion.2
  48.9 2.6 copy.18
  51.5 2.9 copy.19
  54.4 0.7 convert_rsqrt_fusion
  55.2 1.8 fusion.53
  57.0 117.7 %all-reduce.10.cloned.1.call-done = (bf16[128,256]{1,0:T(8,128)(2,1)}, bf16[128,256]{1,0:T(8,128)(2,1)}, bf16[128,256]{1,0:T(8,128)(2,1)}, bf16[128,256]{1,0:T(8...) async-done(((bf16[128,256]{1,0:T(8,128)(2,1)}, bf16[128,256]{1,0:T(8,128)(2,1)}, ...) | async-done | bytes 524304 | tf_op jit(solution)/shard_map/psum | solution.py:12
  174.6 1.6 fusion.37
  176.2 0.0 copy-start.5
  176.2 1.6 convolution_add_fusion.8
  177.9 0.7 copy-done.5
  178.6 0.5 convolution_add_fusion.7
  179.1 0.4 copy-done.16
  179.4 0.5 convolution_add_fusion.6
  179.9 0.4 copy-done.15
  180.3 0.5 convolution_add_fusion.5
  180.7 0.4 copy-done.14
  181.1 0.5 convolution_add_fusion.4
  181.6 0.4 copy-done.13
  182.0 0.5 convolution_add_fusion.3
  182.4 1.1 copy-done.4
  183.5 1.8 fusion.9
  185.4 3.1 fusion.10
  188.5 3.0 fusion.15
  191.5 1.1 fusion.54
  192.7 1.2 convolution_bitcast_fusion.1
  193.9 2.7 fusion.12
  196.5 1.7 copy.29
  198.2 2.8 gather_fusion.2
  201.0 6.8 %fusion.23 = f32[64,256,128]{2,1,0:T(8,128)} fusion(bf16[64,128,256]{2,1,0:T(8,128)(2,1)} %gather_fusion.2, bf16[1,64,128,128]{3,2,1,0:T(8,128)(2,1)S(1)} %copy-done), kind=kOutput, calls=%fused_computation.42 | convolution fusion | flops 536870912 | bytes 14680064 | tf_op jit(solution)/shard_map/lab,laf->lbf/dot_general | solution.py:84
  207.8 9.2 %copy.27 = f32[64,256,128]{1,0,2:T(8,128)} copy(f32[64,256,128]{2,1,0:T(8,128)} %fusion.23) | data formatting | bytes 16777216 | tf_op jit(solution)/shard_map/lab,laf->lbf/dot_general | solution.py:84
  217.0 5.2 fusion
  222.2 2.6 copy.22
  224.8 0.0 all-reduce.8.cloned.1.call-update
  224.8 0.0 all-reduce.6.cloned.1.call-start
  224.8 3.4 fusion.28
  228.3 0.9 copy.30
  229.2 0.0 all-reduce.6.cloned.1.call-update
  229.2 2.7 fusion.29
  231.9 0.8 copy.23
  232.8 4.8 all-to-all-start.1
  237.6 3.4 convolution_add_fusion
  241.0 233.6 %all-reduce.8.cloned.1.call-done = (f32[256,256]{0,1:T(8,128)}, f32[256,256]{1,0:T(8,128)}) async-done(((f32[256,256]{0,1:T(8,128)}, f32[256,256]{1,0:T(8,128)}), (f32[256,256]{0,1:T(8,128)}, f32[256,256]{1,0:T(8,128)})) %all-reduce.8.cloned.1.call-update) | async-done | bytes 524304 | tf_op jit(solution)/shard_map/psum | solution.py:75
  474.6 1.8 copy.24
  476.4 148.1 %all-reduce.6.cloned.1.call-done = bf16[8,128,256]{1,0,2:T(8,128)(2,1)} async-done(((bf16[8,128,256]{1,0,2:T(8,128)(2,1)}), bf16[8,128,256]{1,0,2:T(8,128)(2,1)}) %all-reduce.6.cloned.1.call-update) | async-done | bytes 524304 | tf_op jit(solution)/shard_map/psum | solution.py:91
  624.6 1.3 fusion.46
  625.9 0.1 copy.28
  626.0 1.6 fusion.39
  627.6 3.4 fusion.11
  631.1 0.7 copy.43
  (46 shorter events, 0.1 us)
Async XLA Ops:
  7.2 20.6 %copy-start = (bf16[1,64,128,128]{3,2,1,0:T(8,128)(2,1)S(1)}, bf16[1,64,128,128]{3,2,1,0:T(8,128)(2,1)}, u32[]{:S(2)}) copy-start(bf16[1,64,128,128]{3,2,1,0:T(8,128)(2,1)} %param.17) | copy-start | bytes 6291460
  7.2 16.6 %copy-start.20 = (s32[1,8,64]{2,1,0:T(8,128)S(1)}, s32[1,8,64]{2,1,0:T(8,128)}, u32[]{:S(2)}) copy-start(s32[1,8,64]{2,1,0:T(8,128)} %param.21) | copy-start | bytes 6148
  7.2 15.7 %copy-start.1 = (bf16[2048,256]{1,0:T(8,128)(2,1)S(1)}, bf16[2048,256]{1,0:T(8,128)(2,1)}, u32[]{:S(2)}) copy-start(bf16[2048,256]{1,0:T(8,128)(2,1)} %param.13) | copy-start | bytes 3145732
  7.2 10.0 %copy-start.19 = (s32[1,8]{1,0:T(1,128)S(1)}, s32[1,8]{1,0:T(1,128)}, u32[]{:S(2)}) copy-start(s32[1,8]{1,0:T(1,128)} %param.20) | copy-start | bytes 100
  7.2 17.2 %copy-start.23 = (s32[1,64,2]{1,2,0:T(2,128)S(1)}, s32[1,64,2]{1,2,0:T(2,128)}, u32[]{:S(2)}) copy-start(s32[1,64,2]{1,2,0:T(2,128)} %param.18) | copy-start | bytes 1540
  11.7 173.6 %all-to-all-start = ((bf16[8,64,256]{2,1,0:T(8,128)(2,1)}), bf16[8,64,256]{2,1,0:T(8,128)(2,1)S(1)}, u32[]{:S(2)}, u32[]{:S(2)}) async-start(bf16[8,64,256]{2,1,0:T(8,128)(2,1)} %bitcast.18), calls=%async_computation | async-start | bytes 524288 | tf_op jit(solution)/shard_map/all_to_all | solution.py:53
  17.2 157.4 %all-reduce.10.cloned.1.call-start = ((), (), s32[]{:S(2)}) async-start(), calls=%async_computation.4 | async-start | bytes 1048576 | tf_op jit(solution)/shard_map/psum | solution.py:12
  23.7 450.9 %all-reduce.8.cloned.1.call-start = ((), (), s32[]{:S(2)}) async-start(), calls=%async_computation.3 | async-start | bytes 1048576 | tf_op jit(solution)/shard_map/psum | solution.py:75
  51.5 3.6 copy-start.8
  174.6 1.6 copy-start.18
  176.2 2.4 copy-start.5
  176.2 2.4 copy-start.17
  178.6 0.8 copy-start.16
  179.4 0.8 copy-start.15
  180.3 0.8 copy-start.14
  181.1 0.8 copy-start.13
  182.0 1.6 copy-start.4
  182.0 1.6 copy-start.12
  185.3 3.2 copy-start.7
  185.4 3.2 copy-start.10
  185.4 3.2 copy-start.24
  191.5 1.1 copy-start.2
  191.5 2.3 copy-start.11
  207.8 9.2 %copy-start.22 = (s32[64]{0:T(128)S(1)}, s32[64]{0:T(128)}, u32[]{:S(2)}) copy-start(s32[64]{0:T(128)} %get-tuple-element.44) | copy-start | bytes 772
  222.2 2.7 copy-start.6
  224.8 399.8 %all-reduce.6.cloned.1.call-start = ((), (), s32[]{:S(2)}) async-start(), calls=%async_computation.2 | async-start | bytes 1048576 | tf_op jit(solution)/shard_map/psum | solution.py:91
  229.2 8.4 %copy-start.3 = (bf16[2048,256]{1,0:T(8,128)(2,1)S(1)}, bf16[2048,256]{1,0:T(8,128)(2,1)}, u32[]{:S(2)}) copy-start(bf16[2048,256]{1,0:T(8,128)(2,1)} %copy-done.2) | copy-start | bytes 3145732
  232.8 394.9 %all-to-all-start.1 = ((bf16[8,64,256]{2,1,0:T(8,128)(2,1)}), bf16[8,64,256]{2,1,0:T(8,128)(2,1)S(1)}, u32[]{:S(2)}, u32[]{:S(2)}) async-start(bf16[8,64,256]{2,1,0:T(8,128)(2,1)} %bitcast.32), calls=%async_computation.1 | async-start | bytes 524288 | tf_op jit(solution)/shard_map/all_to_all | solution.py:99
  237.6 390.0 %copy-start.21 = (s32[512]{0:T(512)S(1)}, s32[512]{0:T(512)}, u32[]{:S(2)}) copy-start(s32[512]{0:T(512)} %eq.97) | copy-start | bytes 6148
  626.0 5.1 copy-start.9
Sparse Core Ops, SparseCore 0:
  23.8 150.7 all-reduce.9
  224.9 249.6 all-reduce.7
  478.4 146.1 all-reduce.5
where the time goes:
time: 640 us; the launch traced here: 638 us
  waiting for transfers between devices  499 us (78%)
  matrix products  58.4 us (9%)
  local copies, waits for them, and re-layouts  46.5 us (7%)
  between operations  19 us (3%)
  starting transfers between devices  10.4 us (2%)
    psum x1, waiting for transfers between devices, on_device(): lax.psum((self_part, neighbor_part), ('grp', 'row'))  234 us
    psum x1, waiting for transfers between devices, on_device(): totals = lax.psum(hub_terms.astype(jnp.bfloat16), 'row').astype(jnp.float32)  148 us
    psum x1, waiting for transfers between devices, spread(): return lax.psum(jnp.where(mine, value, jnp.zeros_like(value)), axis)  118 us
  transfers between devices with their start and end apart: 5, of which 3 were waited for; matrix products, arithmetic and copies ran while one was open for 9% of the time, Pallas kernels for 0%

commit v1 on v0

--- a/solution.py
+++ b/solution.py
@@ -72,7 +72,7 @@
     neighbor_part = lax.dot_general(
         aggregated, grad_before, rows_dims, preferred_element_type=jnp.float32
     )
-    grad_self, grad_neighbor = lax.psum((self_part, neighbor_part), ("grp", "row"))
+    grad_self, grad_neighbor = lax.psum(lax.psum((self_part, neighbor_part), "grp"), "row")
     grad_aggregate = (
         lax.dot_general(grad_before, neighbor_weight, cols_dims, preferred_element_type=jnp.float32)
         * scaling

time: 640 us -> 599 us (0.936)
  waiting for transfers between devices: 499 us -> 458 us
    psum x1 -> x2, waiting for transfers between devices: 234 us -> 188 us  [the longest x1 142 us: on_device(): lax.psum(lax.psum((self_part, neighbor_part), 'grp'), 'row')]
  transfers between devices with their start and end apart: 5 -> 6, of which waited for: 3 -> 4; matrix products, arithmetic and copies ran while one was open for 9% -> 10% of each run, Pallas kernels for 0% -> 0%
where the time goes in v1:
time: 599 us; the launch traced here: 597 us
  waiting for transfers between devices  458 us (76%)
  matrix products  58.4 us (10%)
  local copies, waits for them, and re-layouts  47.4 us (8%)
  between operations  19.1 us (3%)
  starting transfers between devices  10.4 us (2%)
    psum x1, waiting for transfers between devices, on_device(): totals = lax.psum(hub_terms.astype(jnp.bfloat16), 'row').astype(jnp.float32)  152 us
    psum x1, waiting for transfers between devices, on_device(): lax.psum(lax.psum((self_part, neighbor_part), 'grp'), 'row')  142 us
    psum x1, waiting for transfers between devices, spread(): return lax.psum(jnp.where(mine, value, jnp.zeros_like(value)), axis)  118 us
    psum x1, waiting for transfers between devices, on_device(): lax.psum((self_part, neighbor_part), 'grp')  45.8 us
  transfers between devices with their start and end apart: 6, of which 4 were waited for; matrix products, arithmetic and copies ran while one was open for 10% of the time, Pallas kernels for 0%

profile of v1, /device:TPU:8, one launch (start us, length us, event | category | flops | bytes accessed | tf_op | source)
XLA Modules:
  0.0 597.3 jit_solution(9831554246677630231)
XLA Ops:
  7.2 0.0 copy-start
  7.2 0.8 compare_select_fusion
  8.1 0.1 reshape.124
  8.2 3.6 gather_fusion.1
  11.7 5.5 all-to-all-start
  17.3 0.7 fusion.52
  23.0 0.8 broadcast_select_fusion
  23.7 0.0 all-reduce.14.cloned.1.call-update
  23.8 0.0 all-reduce.12.cloned.1.call-start
  23.8 0.6 eq.97
  24.5 0.5 slice_bitcast_fusion
  25.0 2.8 gather_fusion
  27.8 6.8 %fusion.25 = f32[64,256,128]{2,1,0:T(8,128)} fusion(bf16[64,128,256]{2,1,0:T(8,128)(2,1)} %gather_fusion, bf16[1,64,128,128]{3,2,1,0:T(8,128)(2,1)S(1)} %copy-done), kind=kOutput, calls=%fused_computation.44 | convolution fusion | flops 536870912 | bytes 14680064 | tf_op jit(solution)/shard_map/lab,lbf->laf/dot_general | solution.py:39
  34.6 9.2 %copy.25 = f32[64,256,128]{1,0,2:T(8,128)} copy(f32[64,256,128]{2,1,0:T(8,128)} %fusion.25) | data formatting | bytes 16777216 | tf_op jit(solution)/shard_map/lab,lbf->laf/dot_general | solution.py:39
  43.8 5.2 fusion.2
  49.0 2.6 copy.18
  51.5 2.9 copy.19
  54.5 0.7 convert_rsqrt_fusion
  55.2 1.8 fusion.53
  57.0 117.7 %all-reduce.14.cloned.1.call-done = (bf16[128,256]{1,0:T(8,128)(2,1)}, bf16[128,256]{1,0:T(8,128)(2,1)}, bf16[128,256]{1,0:T(8,128)(2,1)}, bf16[128,256]{1,0:T(8...) async-done(((bf16[128,256]{1,0:T(8,128)(2,1)}, bf16[128,256]{1,0:T(8,128)(2,1)}, ...) | async-done | bytes 524304 | tf_op jit(solution)/shard_map/psum | solution.py:12
  174.7 1.6 fusion.37
  176.3 1.6 convolution_add_fusion.8
  178.0 0.7 copy-done.5
  178.7 0.5 convolution_add_fusion.7
  179.1 0.4 copy-done.15
  179.5 0.5 convolution_add_fusion.6
  180.0 0.4 copy-done.14
  180.3 0.5 convolution_add_fusion.5
  180.8 0.4 copy-done.13
  181.2 0.5 convolution_add_fusion.4
  181.7 0.4 copy-done.12
  182.0 0.5 convolution_add_fusion.3
  182.5 1.1 copy-done.4
  183.6 1.8 fusion.9
  185.4 3.1 fusion.10
  188.6 3.0 fusion.15
  191.6 1.1 fusion.54
  192.7 1.2 convolution_bitcast_fusion.1
  193.9 2.7 fusion.12
  196.6 1.7 copy.29
  198.3 2.8 gather_fusion.2
  201.1 6.8 %fusion.23 = f32[64,256,128]{2,1,0:T(8,128)} fusion(bf16[64,128,256]{2,1,0:T(8,128)(2,1)} %gather_fusion.2, bf16[1,64,128,128]{3,2,1,0:T(8,128)(2,1)S(1)} %copy-done), kind=kOutput, calls=%fused_computation.42 | convolution fusion | flops 536870912 | bytes 14680064 | tf_op jit(solution)/shard_map/lab,laf->lbf/dot_general | solution.py:84
  207.9 9.2 %copy.27 = f32[64,256,128]{1,0,2:T(8,128)} copy(f32[64,256,128]{2,1,0:T(8,128)} %fusion.23) | data formatting | bytes 16777216 | tf_op jit(solution)/shard_map/lab,laf->lbf/dot_general | solution.py:84
  217.1 5.2 fusion
  222.3 2.5 copy.22
  224.8 0.0 all-reduce.12.cloned.1.call-update
  224.8 0.0 all-reduce.8.cloned.1.call-start
  224.9 3.4 fusion.28
  228.3 0.9 copy.30
  229.2 0.0 all-reduce.8.cloned.1.call-update
  229.3 2.7 fusion.29
  232.0 0.8 copy.23
  232.8 4.8 all-to-all-start.1
  237.7 3.4 convolution_add_fusion
  241.1 45.8 %all-reduce.12.cloned.1.call-done = (f32[256,256]{0,1:T(8,128)}, f32[256,256]{1,0:T(8,128)}) async-done(((f32[256,256]{0,1:T(8,128)}, f32[256,256]{1,0:T(8,128)}), (f32[256,256]{0,1:T(8,128)}, f32[256,256]{1,0:T(8,128)})) %all-reduce.12.cloned.1.call-update) | async-done | bytes 524304 | tf_op jit(solution)/shard_map/psum | solution.py:75
  286.9 0.0 all-reduce.10.cloned.1.call-update
  286.9 152.2 %all-reduce.8.cloned.1.call-done = bf16[8,128,256]{1,0,2:T(8,128)(2,1)} async-done(((bf16[8,128,256]{1,0,2:T(8,128)(2,1)}), bf16[8,128,256]{1,0,2:T(8,128)(2,1)}) %all-reduce.8.cloned.1.call-update) | async-done | bytes 524304 | tf_op jit(solution)/shard_map/psum | solution.py:91
  439.2 1.3 fusion.46
  440.5 0.1 copy.28
  440.6 1.6 fusion.39
  442.2 3.4 fusion.11
  445.6 141.7 %all-reduce.10.cloned.1.call-done = (f32[256,256]{0,1:T(8,128)}, f32[256,256]{1,0:T(8,128)}) async-done(((f32[256,256]{0,1:T(8,128)}, f32[256,256]{1,0:T(8,128)}), (f32[256,256]{0,1:T(8,128)}, f32[256,256]{1,0:T(8,128)})) %all-reduce.10.cloned.1.call-update) | async-done | bytes 524304 | tf_op jit(solution)/shard_map/psum | solution.py:75
  587.3 1.8 copy.24
  589.1 1.7 copy.45
  (47 shorter events, 0.1 us)
Async XLA Ops:
  7.2 20.7 %copy-start = (bf16[1,64,128,128]{3,2,1,0:T(8,128)(2,1)S(1)}, bf16[1,64,128,128]{3,2,1,0:T(8,128)(2,1)}, u32[]{:S(2)}) copy-start(bf16[1,64,128,128]{3,2,1,0:T(8,128)(2,1)} %param.17) | copy-start | bytes 6291460
  7.2 16.6 %copy-start.19 = (s32[1,8,64]{2,1,0:T(8,128)S(1)}, s32[1,8,64]{2,1,0:T(8,128)}, u32[]{:S(2)}) copy-start(s32[1,8,64]{2,1,0:T(8,128)} %param.21) | copy-start | bytes 6148
  7.2 15.8 %copy-start.1 = (bf16[2048,256]{1,0:T(8,128)(2,1)S(1)}, bf16[2048,256]{1,0:T(8,128)(2,1)}, u32[]{:S(2)}) copy-start(bf16[2048,256]{1,0:T(8,128)(2,1)} %param.13) | copy-start | bytes 3145732
  7.2 10.0 %copy-start.18 = (s32[1,8]{1,0:T(1,128)S(1)}, s32[1,8]{1,0:T(1,128)}, u32[]{:S(2)}) copy-start(s32[1,8]{1,0:T(1,128)} %param.20) | copy-start | bytes 100
  7.2 17.3 %copy-start.22 = (s32[1,64,2]{1,2,0:T(2,128)S(1)}, s32[1,64,2]{1,2,0:T(2,128)}, u32[]{:S(2)}) copy-start(s32[1,64,2]{1,2,0:T(2,128)} %param.18) | copy-start | bytes 1540
  11.7 173.7 %all-to-all-start = ((bf16[8,64,256]{2,1,0:T(8,128)(2,1)}), bf16[8,64,256]{2,1,0:T(8,128)(2,1)S(1)}, u32[]{:S(2)}, u32[]{:S(2)}) async-start(bf16[8,64,256]{2,1,0:T(8,128)(2,1)} %bitcast.18), calls=%async_computation | async-start | bytes 524288 | tf_op jit(solution)/shard_map/all_to_all | solution.py:53
  17.2 157.5 %all-reduce.14.cloned.1.call-start = ((), (), s32[]{:S(2)}) async-start(), calls=%async_computation.5 | async-start | bytes 1048576 | tf_op jit(solution)/shard_map/psum | solution.py:12
  23.8 263.1 %all-reduce.12.cloned.1.call-start = ((), (), s32[]{:S(2)}) async-start(), calls=%async_computation.4 | async-start | bytes 1048576 | tf_op jit(solution)/shard_map/psum | solution.py:75
  51.5 3.6 copy-start.8
  174.7 1.6 copy-start.17
  176.3 2.4 copy-start.5
  176.3 2.4 copy-start.16
  178.7 0.8 copy-start.15
  179.5 0.8 copy-start.14
  180.3 0.8 copy-start.13
  181.2 0.8 copy-start.12
  182.0 1.6 copy-start.4
  182.0 1.6 copy-start.11
  185.4 3.2 copy-start.7
  185.4 3.2 copy-start.9
  185.4 3.2 copy-start.23
  191.6 1.1 copy-start.2
  191.6 2.3 copy-start.10
  207.9 9.2 %copy-start.21 = (s32[64]{0:T(128)S(1)}, s32[64]{0:T(128)}, u32[]{:S(2)}) copy-start(s32[64]{0:T(128)} %get-tuple-element.46) | copy-start | bytes 772
  222.2 2.6 copy-start.6
  224.8 214.3 %all-reduce.8.cloned.1.call-start = ((), (), s32[]{:S(2)}) async-start(), calls=%async_computation.2 | async-start | bytes 1048576 | tf_op jit(solution)/shard_map/psum | solution.py:91
  229.3 8.4 %copy-start.3 = (bf16[2048,256]{1,0:T(8,128)(2,1)S(1)}, bf16[2048,256]{1,0:T(8,128)(2,1)}, u32[]{:S(2)}) copy-start(bf16[2048,256]{1,0:T(8,128)(2,1)} %copy-done.2) | copy-start | bytes 3145732
  232.8 209.3 %all-to-all-start.1 = ((bf16[8,64,256]{2,1,0:T(8,128)(2,1)}), bf16[8,64,256]{2,1,0:T(8,128)(2,1)S(1)}, u32[]{:S(2)}, u32[]{:S(2)}) async-start(bf16[8,64,256]{2,1,0:T(8,128)(2,1)} %bitcast.32), calls=%async_computation.1 | async-start | bytes 524288 | tf_op jit(solution)/shard_map/all_to_all | solution.py:99
  237.7 349.7 %all-reduce.10.cloned.1.call-start = ((), (), s32[]{:S(2)}) async-start(), calls=%async_computation.3 | async-start | bytes 1048576 | tf_op jit(solution)/shard_map/psum | solution.py:75
  237.7 204.5 %copy-start.20 = (s32[512]{0:T(512)S(1)}, s32[512]{0:T(512)}, u32[]{:S(2)}) copy-start(s32[512]{0:T(512)} %eq.97) | copy-start | bytes 6148
Sparse Core Ops, SparseCore 0:
  23.9 150.7 all-reduce.13
  224.9 61.9 all-reduce.11
  290.3 148.8 all-reduce.7
  442.8 144.4 all-reduce.9
